TPU v7x, 32 devices: a whole 2x2x4 slice. The times are simulated.
32 devices in a mesh: sector: 8 (over y, x, core), term: 4 (over z).
Axes of the slice: x: 2, y: 2, z: 4, core: 2. Of those that a mesh axis runs over, the one named last changes fastest.
Arguments:
- x_start: float32 [8, 384, 384], P('sector', 'term'), may hold values from -6 to 6
- x_prev: float32 [8, 384, 384], P('sector', 'term'), may hold values from -6 to 6
- precond: float32 [8, 384, 384], P('sector', 'term'), may hold values from 0.5 to 6
- left_env: bfloat16 [256, 384, 384], P(('sector', 'term')), may hold values from -0.20412415 to 1.2041241
- right_env: bfloat16 [256, 384, 384], P(('sector', 'term')), may hold values from -0.20412415 to 1.2041241
- triples: int32 [640, 4], P(('sector', 'term')), may hold values from 0 to 63, as said below
- trip_count: int32 [8, 4], P('sector', 'term'), may hold values from 5 to 20, as said below
- term_coef: float32 [64], replicated, may hold values from 0.25 to 1
- lanczos_beta: float32 [3], replicated, may hold values from 0.3 to 1.2
- block_owner: int32 [8], replicated, may hold values from 0 to 7, each once
Outputs:
- final_vector: float32 [8, 384, 384], P('sector', 'term')
- rayleigh: float32 [3], replicated
Inputs may be any that keep to these rules, and one draw needn't show every extreme that they name: `triples`: Columns: a left slot below 8, a wavefunction block id below 8, a right slot below 8, an operator term below 64. `trip_count`: some device has exactly 20 live triples in every draw. `block_owner`: each sector index holds exactly one block.
All inputs are finite; a program needn't handle non-finite values.
Results may differ from a plain program's by a relative error of at most 0.006.
Values may be sent and summed in bfloat16 or wider, within the bound.
No kernel may reach another device: no remote copies, remote signals or barrier semaphores. Data moves between devices by JAX's collectives and lax.ppermute only.
A program may use at most 64 MiB of HBM per device.

v0:
```python
import math
import jax
import jax.numpy as jnp
from jax import lax
from jax.sharding import PartitionSpec as P

APPS = 3
EPSILON = 1e-06


def local(
    x_start,
    x_prev,
    precond,
    left_env,
    right_env,
    triples,
    trip_count,
    term_coef,
    lanczos_beta,
    block_owner,
):
    sectors = lax.axis_size("sector")
    term_count = lax.axis_size("term")
    block_size = left_env.shape[1]
    share_rows = x_start.shape[1]
    cell_count = sectors * block_size * block_size
    normaliser = 1.0 / math.sqrt(term_count * triples.shape[0])
    live_count = trip_count[0, 0]
    term_match = triples[:, 3:4] == jnp.arange(term_coef.shape[0], dtype=jnp.int32)[None, :]
    coefficient = jnp.sum(jnp.where(term_match, term_coef[None, :], 0.0), axis=1)
    owner_match = triples[:, 1:2] == jnp.arange(sectors, dtype=jnp.int32)[None, :]
    owner_rows = jnp.sum(jnp.where(owner_match, block_owner[None, :], 0), axis=1)

    def own_rows(array):
        return lax.dynamic_slice_in_dim(array, lax.axis_index("term") * share_rows, share_rows, 1)

    current, previous, diagonal = (
        lax.all_gather(x_start, "term", axis=1, tiled=True),
        lax.all_gather(x_prev, "term", axis=1, tiled=True),
        lax.all_gather(precond, "term", axis=1, tiled=True),
    )
    quotients = []
    for position in range(APPS):
        wave_half = current.astype(jnp.bfloat16)
        gathered = lax.all_gather(wave_half, "sector", axis=0, tiled=True)

        def add_triple(triple, accumulated):
            left_block = lax.dynamic_index_in_dim(left_env, triples[triple, 0], 0, keepdims=False)
            wave_block = lax.dynamic_index_in_dim(gathered, owner_rows[triple], 0, keepdims=False)
            right_block = lax.dynamic_index_in_dim(right_env, triples[triple, 2], 0, keepdims=False)
            middle = jnp.dot(left_block, wave_block, preferred_element_type=jnp.float32).astype(
                jnp.bfloat16
            )
            product = jnp.dot(middle, right_block, preferred_element_type=jnp.float32)
            return accumulated + coefficient[triple] * product

        start_sum = jnp.zeros((block_size, block_size), jnp.float32)
        applied = (lax.fori_loop(0, live_count, add_triple, start_sum) * normaliser)[None]
        applied = lax.psum(applied, "term")
        beta_now = lanczos_beta[position]
        cur_own = own_rows(current)
        app_own = own_rows(applied)
        prev_own = own_rows(previous)
        diag_own = own_rows(diagonal)
        diag_square = diag_own * diag_own
        weighted = diag_square * app_own
        weighted_cur = diag_square * cur_own
        sums_all = lax.psum(
            (
                jnp.sum(cur_own * app_own),
                jnp.sum(cur_own * cur_own),
                jnp.sum(weighted * app_own),
                jnp.sum(weighted * cur_own),
                jnp.sum(weighted * prev_own),
                jnp.sum(weighted_cur * cur_own),
                jnp.sum(weighted_cur * prev_own),
                jnp.sum(diag_square * prev_own * prev_own),
            ),
            ("sector", "term"),
        )
        (
            cross_sum,
            self_sum,
            image_image,
            image_current,
            image_previous,
            current_current,
            current_previous,
            previous_previous,
        ) = sums_all
        quotient = cross_sum / self_sum
        square_sum = (
            image_image
            - 2.0 * quotient * image_current
            - 2.0 * beta_now * image_previous
            + quotient * quotient * current_current
            + 2.0 * quotient * beta_now * current_previous
            + beta_now * beta_now * previous_previous
        )
        residual = applied - quotient * current - beta_now * previous
        scaled = diagonal * residual
        following = scaled / jnp.sqrt(square_sum / cell_count + EPSILON)
        previous, current = (current, following)
        quotients.append(quotient)
    return (own_rows(current), jnp.stack(quotients))


def solution(mesh):
    placed = (
        P("sector", "term", None),
        P("sector", "term", None),
        P("sector", "term", None),
        P(("sector", "term"), None, None),
        P(("sector", "term"), None, None),
        P(("sector", "term"), None),
        P("sector", "term"),
        P(),
        P(),
        P(),
    )
    return jax.shard_map(
        local,
        mesh=mesh,
        in_specs=placed,
        out_specs=(P("sector", "term", None), P()),
        check_vma=False,
    )
```

profile of v0, /device:TPU:0, one launch (start us, length us, event | category | flops | bytes accessed | tf_op | source)
XLA Modules:
  0.0 1039.4 jit_solution(10864611968168883217)
XLA Ops:
  7.2 18.5 %all_gather.19 = f32[1,384,384]{2,1,0:T(8,128)S(1)} all-gather(f32[1,96,384]{2,1,0:T(8,128)} %param.16), channel_id=1, replica_groups=mesh['sector'=8,'term'=4] {'term'}, dimensions={1}, use_global_device_ids=true | all-gather | bytes 737280 | tf_op jit(solution)/shard_map/all_gather | solution.py:39
  25.7 0.8 convert_element_type.18
  26.5 0.8 slice_bitcast_fusion
  27.3 0.8 select_reduce_fusion
  28.1 0.7 select_reduce_fusion.1
  28.9 27.8 %all-gather.4.cloned.1.call-done = bf16[8,384,384]{2,1,0:T(8,128)(2,1)} async-done(((bf16[1,384,384]{2,1,0:T(8,128)(2,1)}), bf16[8,384,384]{2,1,0:T(8,128)(2,1)}) %all-gather.4.cloned.1.call-update) | async-done | bytes 2359312 | tf_op jit(solution)/shard_map/all_gather | solution.py:46
  56.8 105.1 %while.30 = (s32[]{:T(128)}, f32[384,384]{1,0:T(8,128)S(1)}, s32[]{:T(128)}, f32[20]{0:T(128)S(1)}, s32[20,4]{0,1:T(4,128)S(1)}, /*index=5*/bf16[8,384,384]{2,1,...) while((s32[]{:T(128)}, f32[384,384]{1,0:T(8,128)S(1)}, ...), condition=%wide.region_3.4_spmd, body=%wide.region_2.3_spmd.sunk | while | flops 226934800 | bytes 2065213 | solution.py:59
  64.8 2.4 fusion.58
  75.3 2.4 fusion.58
  85.7 2.4 fusion.58
  96.1 2.4 fusion.58
  106.6 2.4 fusion.58
  117.0 2.4 fusion.58
  127.5 2.4 fusion.58
  137.9 2.4 fusion.58
  148.4 2.4 fusion.58
  158.8 2.4 fusion.58
  161.9 0.9 multiply_bitcast_fusion.2
  165.4 33.6 %all_gather.18 = f32[1,384,384]{2,1,0:T(8,128)S(1)} all-gather(f32[1,96,384]{2,1,0:T(8,128)S(1)} %copy-done), channel_id=1, replica_groups=mesh['sector'=8,'term'=4] {'term'}, dimensions={1}, use_global_device_ids=true | all-gather | bytes 737280 | tf_op jit(solution)/shard_map/all_gather | solution.py:41
  199.0 16.4 %all_gather.21 = f32[1,384,384]{2,1,0:T(8,128)S(1)} all-gather(f32[1,96,384]{2,1,0:T(8,128)S(1)} %copy-done.1), channel_id=1, replica_groups=mesh['sector'=8,'term'=4] {'term'}, dimensions={1}, use_global_device_ids=true | all-gather | bytes 737280 | tf_op jit(solution)/shard_map/all_gather | solution.py:40
  215.4 97.2 %all-reduce.7.cloned.1.call-done = f32[1,384,384]{2,1,0:T(8,128)} async-done(((f32[1,384,384]{2,1,0:T(8,128)}), f32[1,384,384]{2,1,0:T(8,128)}) %all-reduce.7.cloned.1.call-update) | async-done | bytes 589840 | tf_op jit(solution)/shard_map/psum | solution.py:60
  312.6 1.7 fusion.39
  314.3 42.7 %all-reduce.2 = (f32[]{:T(128)}, f32[]{:T(128)}, f32[]{:T(128)}, f32[]{:T(128)}, f32[]{:T(128)}, /*index=5*/f32[]{:T(128)}, f32[]{:T(128)}, f32[]{:T(128)}) all-reduce(f32[]{:T(128)} %get-tuple-element.167, f32[]{:T(128)} %get-tuple-element.166, f32[]{:T(128)} %get-tuple-element.168, ...), channel_id=1, replica_groups=mesh['sector'=8,'term'=4] {'sector','term'}, use_global_device_ids=true, to_apply=%region_10.11 | all-reduce | flops 8 | bytes 64 | tf_op jit(solution)/shard_map/psum | solution.py:69
  362.8 2.5 fusion.41
  365.4 29.6 %all-gather.6.cloned.1.call-done = bf16[8,384,384]{2,1,0:T(8,128)(2,1)} async-done(((bf16[1,384,384]{2,1,0:T(8,128)(2,1)}), bf16[8,384,384]{2,1,0:T(8,128)(2,1)}) %all-gather.6.cloned.1.call-update) | async-done | bytes 2359312 | tf_op jit(solution)/shard_map/all_gather | solution.py:46
  395.1 105.1 %while.31 = (s32[]{:T(128)}, f32[384,384]{1,0:T(8,128)S(1)}, s32[]{:T(128)}, f32[20]{0:T(128)S(1)}, s32[20,4]{0,1:T(4,128)S(1)}, /*index=5*/bf16[8,384,384]{2,1,...) while((s32[]{:T(128)}, f32[384,384]{1,0:T(8,128)S(1)}, ...), condition=%wide.region_22.23_spmd, body=%wide.region_21.22_spmd.sunk | while | flops 226934800 | bytes 2065213 | solution.py:59
  403.1 2.4 fusion.62
  413.5 2.4 fusion.62
  423.9 2.4 fusion.62
  434.4 2.4 fusion.62
  444.8 2.4 fusion.62
  455.3 2.4 fusion.62
  465.7 2.4 fusion.62
  476.2 2.4 fusion.62
  486.6 2.4 fusion.62
  497.0 2.4 fusion.62
  500.1 0.9 multiply_bitcast_fusion.1
  503.8 140.3 %all-reduce.9.cloned.1.call-done = f32[1,384,384]{2,1,0:T(8,128)} async-done(((f32[1,384,384]{2,1,0:T(8,128)}), f32[1,384,384]{2,1,0:T(8,128)}) %all-reduce.9.cloned.1.call-update) | async-done | bytes 589840 | tf_op jit(solution)/shard_map/psum | solution.py:60
  644.1 1.7 multiply_reduce_fusion.7
  645.8 40.3 %all-reduce.1 = (f32[]{:T(128)}, f32[]{:T(128)}, f32[]{:T(128)}, f32[]{:T(128)}, f32[]{:T(128)}, /*index=5*/f32[]{:T(128)}, f32[]{:T(128)}) all-reduce(f32[]{:T(128)} %get-tuple-element.159, f32[]{:T(128)} %get-tuple-element.160, f32[]{:T(128)} %get-tuple-element.170, ...), channel_id=1, replica_groups=mesh['sector'=8,'term'=4] {'sector','term'}, use_global_device_ids=true, to_apply=%region_29.30 | all-reduce | flops 7 | bytes 56 | tf_op jit(solution)/shard_map/psum | solution.py:69
  691.3 2.6 fusion.40
  694.0 28.5 %all-gather.8.cloned.1.call-done = bf16[8,384,384]{2,1,0:T(8,128)(2,1)} async-done(((bf16[1,384,384]{2,1,0:T(8,128)(2,1)}), bf16[8,384,384]{2,1,0:T(8,128)(2,1)}) %all-gather.8.cloned.1.call-update) | async-done | bytes 2359312 | tf_op jit(solution)/shard_map/all_gather | solution.py:46
  722.5 110.6 %while.32 = (s32[]{:T(128)}, f32[384,384]{1,0:T(8,128)S(1)}, s32[]{:T(128)}, f32[20]{0:T(128)S(1)}, s32[20,4]{0,1:T(4,128)S(1)}, /*index=5*/bf16[8,384,384]{2,1,...) while((s32[]{:T(128)}, f32[384,384]{1,0:T(8,128)S(1)}, ...), condition=%wide.region_39.40_spmd, body=%wide.region_38.39_spmd.sunk | while | flops 226934800 | bytes 2065213 | solution.py:59
  727.6 0.7 dynamic_slice.282
  731.0 2.5 fusion.66
  738.6 0.7 dynamic_slice.282
  742.0 2.5 fusion.66
  752.3 0.7 dynamic_slice.283
  753.0 2.5 fusion.66
  764.0 2.5 fusion.66
  771.6 0.7 dynamic_slice.282
  775.0 2.5 fusion.66
  782.6 0.7 dynamic_slice.282
  786.0 2.5 fusion.66
  796.3 0.7 dynamic_slice.283
  797.0 2.5 fusion.66
  808.0 2.5 fusion.66
  819.0 2.5 fusion.66
  830.0 2.5 fusion.66
  833.1 0.9 multiply_bitcast_fusion
  836.4 146.3 %all-reduce.11.cloned.1.call-done = f32[1,384,384]{2,1,0:T(8,128)} async-done(((f32[1,384,384]{2,1,0:T(8,128)}), f32[1,384,384]{2,1,0:T(8,128)}) %all-reduce.11.cloned.1.call-update) | async-done | bytes 589840 | tf_op jit(solution)/shard_map/psum | solution.py:60
  982.7 1.7 multiply_reduce_fusion
  984.3 40.3 %all-reduce = (f32[]{:T(128)}, f32[]{:T(128)}, f32[]{:T(128)}, f32[]{:T(128)}, f32[]{:T(128)}, /*index=5*/f32[]{:T(128)}, f32[]{:T(128)}) all-reduce(f32[]{:T(128)} %get-tuple-element.152, f32[]{:T(128)} %get-tuple-element.153, f32[]{:T(128)} %get-tuple-element.169, ...), channel_id=1, replica_groups=mesh['sector'=8,'term'=4] {'sector','term'}, use_global_device_ids=true, to_apply=%region_46.47 | all-reduce | flops 7 | bytes 56 | tf_op jit(solution)/shard_map/psum | solution.py:69
  1030.3 2.2 multiply_divide_fusion.2
  (109 shorter events, 53.0 us)
Async XLA Ops:
  7.2 49.6 %copy-start.2 = (s32[20,4]{0,1:T(4,128)S(1)}, s32[20,4]{0,1:T(4,128)}, u32[]{:S(2)}) copy-start(s32[20,4]{0,1:T(4,128)} %param.21) | copy-start | bytes 964
  7.2 49.5 %all-gather.4.cloned.1.call-start = ((), (), s32[]{:S(2)}) async-start(), calls=%async_computation | async-start | bytes 2654208 | tf_op jit(solution)/shard_map/all_gather | solution.py:46
  26.5 286.1 %all-reduce.7.cloned.1.call-start = ((), (), s32[]{:S(2)}) async-start(), calls=%async_computation.1 | async-start | bytes 1179648 | tf_op jit(solution)/shard_map/psum | solution.py:60
  56.8 106.1 %copy-start.3 = (f32[3]{0:T(128)S(1)}, f32[3]{0:T(128)}, u32[]{:S(2)}) copy-start(f32[3]{0:T(128)} %param.24) | copy-start | bytes 40
  56.8 108.6 %copy-start = (f32[1,96,384]{2,1,0:T(8,128)S(1)}, f32[1,96,384]{2,1,0:T(8,128)}, u32[]{:S(2)}) copy-start(f32[1,96,384]{2,1,0:T(8,128)} %param.18) | copy-start | bytes 442372
  161.9 37.1 %copy-start.1 = (f32[1,96,384]{2,1,0:T(8,128)S(1)}, f32[1,96,384]{2,1,0:T(8,128)}, u32[]{:S(2)}) copy-start(f32[1,96,384]{2,1,0:T(8,128)} %param.17) | copy-start | bytes 442372
  162.8 232.2 %all-gather.6.cloned.1.call-start = ((), (), s32[]{:S(2)}) async-start(), calls=%async_computation.2 | async-start | bytes 2654208 | tf_op jit(solution)/shard_map/all_gather | solution.py:46
  365.3 278.8 %all-reduce.9.cloned.1.call-start = ((), (), s32[]{:S(2)}) async-start(), calls=%async_computation.3 | async-start | bytes 1179648 | tf_op jit(solution)/shard_map/psum | solution.py:60
  501.0 221.4 %all-gather.8.cloned.1.call-start = ((), (), s32[]{:S(2)}) async-start(), calls=%async_computation.4 | async-start | bytes 2654208 | tf_op jit(solution)/shard_map/all_gather | solution.py:46
  693.9 288.7 %all-reduce.11.cloned.1.call-start = ((), (), s32[]{:S(2)}) async-start(), calls=%async_computation.5 | async-start | bytes 1179648 | tf_op jit(solution)/shard_map/psum | solution.py:60
Sparse Core Ops, SparseCore 0:
  26.6 30.0 all-gather.3
  162.9 149.6 all-reduce.6
  365.5 29.5 all-gather.5
  501.1 142.9 all-reduce.8
  694.0 28.3 all-gather.7
  834.1 148.4 all-reduce.10
where the time goes:
time: 1050 us; the launch traced here: 1040 us
  waiting for transfers between devices  470 us (45%)
  blocking collectives  192 us (18%)
  loops' own time  192 us (18%)
  matrix products  73.7 us (7%)
  local copies, waits for them, and re-layouts  56.9 us (5%)
  between operations  37.2 us (4%)
  other arithmetic  17.8 us (2%)
    psum x3, waiting for transfers between devices, local(): applied = lax.psum(applied, 'term')  384 us
    another operation x3, loops' own time, local(): lax.fori_loop(0, live_count, add_triple, start_sum) * normaliser  192 us
    psum x3, blocking collectives, local(): lax.psum((jnp.sum(cur_own * app_own), jnp.sum(cur_own * cur_own), jnp.sum...  123 us
    all_gather x3, waiting for transfers between devices, local(): gathered = lax.all_gather(wave_half, 'sector', axis=0, tiled=True)  86 us
    dot_general x30, matrix products, add_triple(): product = jnp.dot(middle, right_block, preferred_element_type=jnp.float32)  73.7 us
    all_gather x1, blocking collectives, local(): lax.all_gather(precond, 'term', axis=1, tiled=True)  33.6 us
  transfers between devices with their start and end apart: 6, of which 6 were waited for; matrix products, arithmetic and copies ran while one was open for 0% of the time, Pallas kernels for 0%

commit v1 on v0

--- a/solution.py
+++ b/solution.py
@@ -57,7 +57,11 @@
 
         start_sum = jnp.zeros((block_size, block_size), jnp.float32)
         applied = (lax.fori_loop(0, live_count, add_triple, start_sum) * normaliser)[None]
-        applied = lax.psum(applied, "term")
+        applied = applied
+        for hop in (1, 2):
+            applied = applied + lax.ppermute(
+                applied, "term", [(dev, dev ^ hop) for dev in range(4)]
+            )
         beta_now = lanczos_beta[position]
         cur_own = own_rows(current)
         app_own = own_rows(applied)

time: 1050 us -> 1050 us (level)
  waiting for transfers between devices: 470 us -> 142 us
  blocking collectives: 192 us -> 459 us
  starting transfers between devices: 0.25 us -> 68.7 us
    psum x3 -> x0, waiting for transfers between devices: 384 us -> none  [local(): applied = lax.psum(applied, 'term')]
    psum x3, blocking collectives: 123 us -> 403 us  [local(): lax.psum((jnp.sum(cur_own * app_own), jnp.sum(cur_own * cur_own), jnp.sum...]
    ppermute x0 -> x6, starting transfers between devices: none -> 68.6 us  [local(): lax.ppermute(applied, 'term', [(dev, dev ^ hop) for dev in range(4)])]
    ppermute x0 -> x6, waiting for transfers between devices: none -> 52.7 us  [local(): lax.ppermute(applied, 'term', [(dev, dev ^ hop) for dev in range(4)])]
    all_gather x1, blocking collectives: 33.6 us -> 22.5 us  [local(): lax.all_gather(precond, 'term', axis=1, tiled=True)]
  transfers between devices with their start and end apart: 6 -> 9, of which waited for: 6 -> 8; matrix products, arithmetic and copies ran while one was open for 0% -> 0% of each run, Pallas kernels for 0% -> 0%
where the time goes in v1:
time: 1050 us; the launch traced here: 1040 us
  blocking collectives  459 us (44%)
  loops' own time  192 us (18%)
  waiting for transfers between devices  142 us (14%)
  matrix products  73.7 us (7%)
  starting transfers between devices  68.7 us (7%)
  local copies, waits for them, and re-layouts  56.9 us (5%)
  between operations  37.3 us (4%)
    psum x3, blocking collectives, local(): lax.psum((jnp.sum(cur_own * app_own), jnp.sum(cur_own * cur_own), jnp.sum...  403 us
    another operation x3, loops' own time, local(): lax.fori_loop(0, live_count, add_triple, start_sum) * normaliser  192 us
    all_gather x3, waiting for transfers between devices, local(): gathered = lax.all_gather(wave_half, 'sector', axis=0, tiled=True)  89.1 us
    dot_general x30, matrix products, add_triple(): product = jnp.dot(middle, right_block, preferred_element_type=jnp.float32)  73.7 us
    ppermute x6, starting transfers between devices, local(): lax.ppermute(applied, 'term', [(dev, dev ^ hop) for dev in range(4)])  68.6 us
    ppermute x6, waiting for transfers between devices, local(): lax.ppermute(applied, 'term', [(dev, dev ^ hop) for dev in range(4)])  52.7 us
    all_gather x1, blocking collectives, local(): lax.all_gather(precond, 'term', axis=1, tiled=True)  22.5 us
  transfers between devices with their start and end apart: 9, of which 8 were waited for; matrix products, arithmetic and copies ran while one was open for 0% of the time, Pallas kernels for 0%

profile of v1, /device:TPU:0, one launch (start us, length us, event | category | flops | bytes accessed | tf_op | source)
XLA Modules:
  0.0 1039.7 jit_solution(1599666440263608965)
XLA Ops:
  7.2 18.5 %all_gather.19 = f32[1,384,384]{2,1,0:T(8,128)S(1)} all-gather(f32[1,96,384]{2,1,0:T(8,128)} %param.16), channel_id=1, replica_groups=mesh['sector'=8,'term'=4] {'term'}, dimensions={1}, use_global_device_ids=true | all-gather | bytes 737280 | tf_op jit(solution)/shard_map/all_gather | solution.py:39
  25.7 0.8 convert_element_type.18
  26.5 0.8 slice_bitcast_fusion
  27.3 0.8 select_reduce_fusion
  28.1 0.7 select_reduce_fusion.1
  28.9 27.8 %all-gather.4.cloned.1.call-done = bf16[8,384,384]{2,1,0:T(8,128)(2,1)} async-done(((bf16[1,384,384]{2,1,0:T(8,128)(2,1)}), bf16[8,384,384]{2,1,0:T(8,128)(2,1)}) %all-gather.4.cloned.1.call-update) | async-done | bytes 2359312 | tf_op jit(solution)/shard_map/all_gather | solution.py:46
  56.8 105.1 %while.30 = (s32[]{:T(128)}, f32[384,384]{1,0:T(8,128)S(1)}, s32[]{:T(128)}, f32[20]{0:T(128)S(1)}, s32[20,4]{0,1:T(4,128)S(1)}, /*index=5*/bf16[8,384,384]{2,1,...) while((s32[]{:T(128)}, f32[384,384]{1,0:T(8,128)S(1)}, ...), condition=%wide.region_3.4_spmd, body=%wide.region_2.3_spmd.sunk | while | flops 226934800 | bytes 2065213 | solution.py:59
  64.8 2.4 fusion.61
  75.2 2.4 fusion.61
  85.6 2.4 fusion.61
  96.1 2.4 fusion.61
  106.5 2.4 fusion.61
  117.0 2.4 fusion.61
  127.4 2.4 fusion.61
  137.9 2.4 fusion.61
  148.3 2.4 fusion.61
  158.7 2.4 fusion.61
  161.9 22.4 %collective-permute-start = (f32[1,384,384]{2,1,0:T(8,128)S(1)}, f32[1,384,384]{2,1,0:T(8,128)S(1)}, u32[]{:S(2)}, u32[]{:S(2)}) collective-permute-start(f32[1,384,384]{2,1,0:T(8,128)S(1)} %multiply_bitcast_fusion.2), channel_id=1, source_target_pairs={{0,1},{1,0},{2,3},{3,2},{4,5},{5,4},{6,7},{7,6},{8,9},{9,8},{10,11... | collective-permute-start | bytes 1769480 | tf_op jit(solution)/shard_map/ppermute | solution.py:62
  184.4 7.9 collective-permute-done
  195.1 22.5 %all_gather.18 = f32[1,384,384]{2,1,0:T(8,128)S(1)} all-gather(f32[1,96,384]{2,1,0:T(8,128)S(1)} %copy-done), channel_id=1, replica_groups=mesh['sector'=8,'term'=4] {'term'}, dimensions={1}, use_global_device_ids=true | all-gather | bytes 737280 | tf_op jit(solution)/shard_map/all_gather | solution.py:41
  217.6 15.1 %all_gather.21 = f32[1,384,384]{2,1,0:T(8,128)S(1)} all-gather(f32[1,96,384]{2,1,0:T(8,128)S(1)} %copy-done.1), channel_id=1, replica_groups=mesh['sector'=8,'term'=4] {'term'}, dimensions={1}, use_global_device_ids=true | all-gather | bytes 737280 | tf_op jit(solution)/shard_map/all_gather | solution.py:40
  232.8 0.8 fusion.39
  233.6 136.6 %all-reduce.2 = (f32[]{:T(128)}, f32[]{:T(128)}, f32[]{:T(128)}, f32[]{:T(128)}, f32[]{:T(128)}, /*index=5*/f32[]{:T(128)}, f32[]{:T(128)}, f32[]{:T(128)}) all-reduce(f32[]{:T(128)} %get-tuple-element.167, f32[]{:T(128)} %get-tuple-element.166, f32[]{:T(128)} %get-tuple-element.168, ...), channel_id=1, replica_groups=mesh['sector'=8,'term'=4] {'sector','term'}, use_global_device_ids=true, to_apply=%region_9.10 | all-reduce | flops 8 | bytes 64 | tf_op jit(solution)/shard_map/psum | solution.py:73
  376.0 1.5 fusion.44
  377.6 30.3 %all-gather.6.cloned.1.call-done = bf16[8,384,384]{2,1,0:T(8,128)(2,1)} async-done(((bf16[1,384,384]{2,1,0:T(8,128)(2,1)}), bf16[8,384,384]{2,1,0:T(8,128)(2,1)}) %all-gather.6.cloned.1.call-update) | async-done | bytes 2359312 | tf_op jit(solution)/shard_map/all_gather | solution.py:46
  407.9 105.1 %while.31 = (s32[]{:T(128)}, f32[384,384]{1,0:T(8,128)S(1)}, s32[]{:T(128)}, f32[20]{0:T(128)S(1)}, s32[20,4]{0,1:T(4,128)S(1)}, /*index=5*/bf16[8,384,384]{2,1,...) while((s32[]{:T(128)}, f32[384,384]{1,0:T(8,128)S(1)}, ...), condition=%wide.region_21.22_spmd, body=%wide.region_20.21_spmd.sunk | while | flops 226934800 | bytes 2065213 | solution.py:59
  415.9 2.4 fusion.65
  426.3 2.4 fusion.65
  436.8 2.4 fusion.65
  447.2 2.4 fusion.65
  457.7 2.4 fusion.65
  468.1 2.4 fusion.65
  478.6 2.4 fusion.65
  489.0 2.4 fusion.65
  499.4 2.4 fusion.65
  509.9 2.4 fusion.65
  513.0 22.4 %collective-permute-start.2 = (f32[1,384,384]{2,1,0:T(8,128)S(1)}, f32[1,384,384]{2,1,0:T(8,128)S(1)}, u32[]{:S(2)}, u32[]{:S(2)}) collective-permute-start(f32[1,384,384]{2,1,0:T(8,128)S(1)} %multiply_bitcast_fusion.1), channel_id=1, source_target_pairs={{0,1},{1,0},{2,3},{3,2},{4,5},{5,4},{6,7},{7,6},{8,9},{9,8},{10,11... | collective-permute-start | bytes 1769480 | tf_op jit(solution)/shard_map/ppermute | solution.py:62
  535.5 7.9 collective-permute-done.2
  546.3 14.3 %collective-permute-done.3 = f32[1,384,384]{2,1,0:T(8,128)S(1)} collective-permute-done((f32[1,384,384]{2,1,0:T(8,128)S(1)}, f32[1,384,384]{2,1,0:T(8,128)S(1)}, u32[]{:S(2)}, u32[]{:S(2)}) %collective-permute-start.3) | collective-permute-done | bytes 589856 | tf_op jit(solution)/shard_map/ppermute | solution.py:62
  560.6 0.8 multiply_reduce_fusion.7
  561.4 131.1 %all-reduce.1 = (f32[]{:T(128)}, f32[]{:T(128)}, f32[]{:T(128)}, f32[]{:T(128)}, f32[]{:T(128)}, /*index=5*/f32[]{:T(128)}, f32[]{:T(128)}) all-reduce(f32[]{:T(128)} %get-tuple-element.159, f32[]{:T(128)} %get-tuple-element.160, f32[]{:T(128)} %get-tuple-element.170, ...), channel_id=1, replica_groups=mesh['sector'=8,'term'=4] {'sector','term'}, use_global_device_ids=true, to_apply=%region_27.28 | all-reduce | flops 7 | bytes 56 | tf_op jit(solution)/shard_map/psum | solution.py:73
  697.8 1.5 fusion.43
  699.3 31.0 %all-gather.8.cloned.1.call-done = bf16[8,384,384]{2,1,0:T(8,128)(2,1)} async-done(((bf16[1,384,384]{2,1,0:T(8,128)(2,1)}), bf16[8,384,384]{2,1,0:T(8,128)(2,1)}) %all-gather.8.cloned.1.call-update) | async-done | bytes 2359312 | tf_op jit(solution)/shard_map/all_gather | solution.py:46
  730.4 110.6 %while.32 = (s32[]{:T(128)}, f32[384,384]{1,0:T(8,128)S(1)}, s32[]{:T(128)}, f32[20]{0:T(128)S(1)}, s32[20,4]{0,1:T(4,128)S(1)}, /*index=5*/bf16[8,384,384]{2,1,...) while((s32[]{:T(128)}, f32[384,384]{1,0:T(8,128)S(1)}, ...), condition=%wide.region_37.38_spmd, body=%wide.region_36.37_spmd.sunk | while | flops 226934800 | bytes 2065213 | solution.py:59
  738.9 2.5 fusion.69
  749.2 0.7 dynamic_slice.283
  749.9 2.5 fusion.69
  757.5 0.7 dynamic_slice.282
  760.9 2.5 fusion.69
  771.2 0.7 dynamic_slice.283
  771.9 2.5 fusion.69
  782.2 0.7 dynamic_slice.283
  782.9 2.5 fusion.69
  793.9 2.5 fusion.69
  804.9 2.5 fusion.69
  815.9 2.5 fusion.69
  826.9 2.5 fusion.69
  837.9 2.5 fusion.69
  841.1 23.5 %collective-permute-start.4 = (f32[1,384,384]{2,1,0:T(8,128)S(1)}, f32[1,384,384]{2,1,0:T(8,128)S(1)}, u32[]{:S(2)}, u32[]{:S(2)}) collective-permute-start(f32[1,384,384]{2,1,0:T(8,128)S(1)} %multiply_bitcast_fusion), channel_id=1, source_target_pairs={{0,1},{1,0},{2,3},{3,2},{4,5},{5,4},{6,7},{7,6},{8,9},{9,8},{10,11... | collective-permute-start | bytes 1769480 | tf_op jit(solution)/shard_map/ppermute | solution.py:62
  864.6 7.9 collective-permute-done.4
  875.0 14.8 %collective-permute-done.5 = f32[1,384,384]{2,1,0:T(8,128)S(1)} collective-permute-done((f32[1,384,384]{2,1,0:T(8,128)S(1)}, f32[1,384,384]{2,1,0:T(8,128)S(1)}, u32[]{:S(2)}, u32[]{:S(2)}) %collective-permute-start.5) | collective-permute-done | bytes 589856 | tf_op jit(solution)/shard_map/ppermute | solution.py:62
  889.8 0.8 multiply_reduce_fusion
  890.6 135.6 %all-reduce = (f32[]{:T(128)}, f32[]{:T(128)}, f32[]{:T(128)}, f32[]{:T(128)}, f32[]{:T(128)}, /*index=5*/f32[]{:T(128)}, f32[]{:T(128)}) all-reduce(f32[]{:T(128)} %get-tuple-element.152, f32[]{:T(128)} %get-tuple-element.153, f32[]{:T(128)} %get-tuple-element.169, ...), channel_id=1, replica_groups=mesh['sector'=8,'term'=4] {'sector','term'}, use_global_device_ids=true, to_apply=%region_43.44 | all-reduce | flops 7 | bytes 56 | tf_op jit(solution)/shard_map/psum | solution.py:73
  1031.4 1.3 multiply_divide_fusion.2
  (118 shorter events, 55.0 us)
Async XLA Ops:
  7.2 49.6 %copy-start.2 = (s32[20,4]{0,1:T(4,128)S(1)}, s32[20,4]{0,1:T(4,128)}, u32[]{:S(2)}) copy-start(s32[20,4]{0,1:T(4,128)} %param.21) | copy-start | bytes 964
  7.2 49.5 %all-gather.4.cloned.1.call-start = ((), (), s32[]{:S(2)}) async-start(), calls=%async_computation | async-start | bytes 2654208 | tf_op jit(solution)/shard_map/all_gather | solution.py:46
  26.5 381.4 %all-gather.6.cloned.1.call-start = ((), (), s32[]{:S(2)}) async-start(), calls=%async_computation.1 | async-start | bytes 2654208 | tf_op jit(solution)/shard_map/all_gather | solution.py:46
  161.8 30.5 %copy-start.3 = (f32[3]{0:T(128)S(1)}, f32[3]{0:T(128)}, u32[]{:S(2)}) copy-start(f32[3]{0:T(128)} %param.24) | copy-start | bytes 40
  161.9 33.3 %copy-start = (f32[1,96,384]{2,1,0:T(8,128)S(1)}, f32[1,96,384]{2,1,0:T(8,128)}, u32[]{:S(2)}) copy-start(f32[1,96,384]{2,1,0:T(8,128)} %param.18) | copy-start | bytes 442372
  161.9 55.8 %copy-start.1 = (f32[1,96,384]{2,1,0:T(8,128)S(1)}, f32[1,96,384]{2,1,0:T(8,128)}, u32[]{:S(2)}) copy-start(f32[1,96,384]{2,1,0:T(8,128)} %param.17) | copy-start | bytes 442372
  161.9 30.3 %collective-permute-start = (f32[1,384,384]{2,1,0:T(8,128)S(1)}, f32[1,384,384]{2,1,0:T(8,128)S(1)}, u32[]{:S(2)}, u32[]{:S(2)}) collective-permute-start(f32[1,384,384]{2,1,0:T(8,128)S(1)} %multiply_bitcast_fusion.2), channel_id=1, source_target_pairs={{0,1},{1,0},{2,3},{3,2},{4,5},{5,4},{6,7},{7,6},{8,9},{9,8},{10,11... | collective-permute-start | bytes 1769480 | tf_op jit(solution)/shard_map/ppermute | solution.py:62
  192.3 40.4 %collective-permute-start.1 = (f32[1,384,384]{2,1,0:T(8,128)S(1)}, f32[1,384,384]{2,1,0:T(8,128)S(1)}, u32[]{:S(2)}, u32[]{:S(2)}) collective-permute-start(f32[1,384,384]{2,1,0:T(8,128)S(1)} %fusion.40), channel_id=1, source_target_pairs={{0,2},{1,3},{2,0},{3,1},{4,6},{5,7},{6,4},{7,5},{8,10},{9,11},{10,... | collective-permute-start | bytes 1769480 | tf_op jit(solution)/shard_map/ppermute | solution.py:62
  377.6 352.8 %all-gather.8.cloned.1.call-start = ((), (), s32[]{:S(2)}) async-start(), calls=%async_computation.2 | async-start | bytes 2654208 | tf_op jit(solution)/shard_map/all_gather | solution.py:46
  513.0 30.3 %collective-permute-start.2 = (f32[1,384,384]{2,1,0:T(8,128)S(1)}, f32[1,384,384]{2,1,0:T(8,128)S(1)}, u32[]{:S(2)}, u32[]{:S(2)}) collective-permute-start(f32[1,384,384]{2,1,0:T(8,128)S(1)} %multiply_bitcast_fusion.1), channel_id=1, source_target_pairs={{0,1},{1,0},{2,3},{3,2},{4,5},{5,4},{6,7},{7,6},{8,9},{9,8},{10,11... | collective-permute-start | bytes 1769480 | tf_op jit(solution)/shard_map/ppermute | solution.py:62
  543.4 17.2 %collective-permute-start.3 = (f32[1,384,384]{2,1,0:T(8,128)S(1)}, f32[1,384,384]{2,1,0:T(8,128)S(1)}, u32[]{:S(2)}, u32[]{:S(2)}) collective-permute-start(f32[1,384,384]{2,1,0:T(8,128)S(1)} %fusion.41), channel_id=1, source_target_pairs={{0,2},{1,3},{2,0},{3,1},{4,6},{5,7},{6,4},{7,5},{8,10},{9,11},{10,... | collective-permute-start | bytes 1769480 | tf_op jit(solution)/shard_map/ppermute | solution.py:62
  841.1 31.4 %collective-permute-start.4 = (f32[1,384,384]{2,1,0:T(8,128)S(1)}, f32[1,384,384]{2,1,0:T(8,128)S(1)}, u32[]{:S(2)}, u32[]{:S(2)}) collective-permute-start(f32[1,384,384]{2,1,0:T(8,128)S(1)} %multiply_bitcast_fusion), channel_id=1, source_target_pairs={{0,1},{1,0},{2,3},{3,2},{4,5},{5,4},{6,7},{7,6},{8,9},{9,8},{10,11... | collective-permute-start | bytes 1769480 | tf_op jit(solution)/shard_map/ppermute | solution.py:62
  872.6 17.2 %collective-permute-start.5 = (f32[1,384,384]{2,1,0:T(8,128)S(1)}, f32[1,384,384]{2,1,0:T(8,128)S(1)}, u32[]{:S(2)}, u32[]{:S(2)}) collective-permute-start(f32[1,384,384]{2,1,0:T(8,128)S(1)} %fusion.42), channel_id=1, source_target_pairs={{0,2},{1,3},{2,0},{3,1},{4,6},{5,7},{6,4},{7,5},{8,10},{9,11},{10,... | collective-permute-start | bytes 1769480 | tf_op jit(solution)/shard_map/ppermute | solution.py:62
Sparse Core Ops, SparseCore 0:
  26.6 30.0 all-gather.3
  377.7 30.1 all-gather.5
  699.5 30.8 all-gather.7
